TPU v7x, 32 devices: a whole 2x2x4 slice. The times are simulated.
32 devices in a mesh: pairs: 8 (over z, x), hours: 4 (over y, core).
Axes of the slice: x: 2, y: 2, z: 4, core: 2. Of those that a mesh axis runs over, the one named last changes fastest.
Arguments:
- records: bfloat16 [1024, 4, 3600], P('pairs', 'hours'), may hold values from -100 to 100
- usable: int32 [1024, 4], P('pairs', 'hours'), may hold values from 0 to 1, as said below
- pair_blocks: int32 [8, 2], P('pairs'), may hold values from 0 to 7
Outputs:
- correlations: float32 [8, 128, 128, 256], P('pairs', 'hours')
Inputs may be any that keep to these rules, and one draw needn't show every extreme that they name: Some stations are usable in no hour at all. `pair_blocks`: each row names two station blocks; a block may appear in many rows and both entries may be equal.
All inputs are finite; a program needn't handle non-finite values.
Results may differ from a plain program's by a relative error of at most 0.0071.
Values may be sent and summed in bfloat16 or wider, within the bound.
A program may use at most 128 MiB of HBM per device.

v0:
```python
import functools
import math

import jax
import jax.numpy as jnp
import numpy as np
from jax import lax
from jax.experimental import pallas as pl
from jax.experimental.pallas import tpu as pltpu
from jax.sharding import PartitionSpec as P

L = 3600
F = 512
W = 32
F0 = 64
LAGS = 256
EXTENT = F + 2 * W
HALF = L // 2
HE = EXTENT // 2
HF = F // 2
CORES = 2
MESH = pl.DeviceIdType.MESH


def cos_sin(phases, length, scale):
    angles = np.float32(2.0 * math.pi / length) * (phases % length).astype(np.float32)
    wide = angles.astype(np.float64)
    scale = np.float32(scale)
    return np.cos(wide).astype(np.float32) * scale, -np.sin(wide).astype(np.float32) * scale


CHUNK = 128
CHUNKS = F // CHUNK


def spectrum_tables():
    bins = F0 - W + np.arange(EXTENT)
    c, q = cos_sin(bins[:, None] * np.arange(HALF)[None, :], L, 1.0 / math.sqrt(L))
    even = np.concatenate([c[0::2], q[0::2]], axis=0)
    odd = np.concatenate([c[1::2], q[1::2]], axis=0)
    return even.astype(jnp.bfloat16), odd.astype(jnp.bfloat16)


def window_ones():
    source = np.concatenate([np.arange(0, EXTENT, 2), np.arange(1, EXTENT, 2)])
    target = np.concatenate([np.arange(0, F, 2), np.arange(1, F, 2)])
    gap = source[None, :] - target[:, None]
    return ((gap >= 0) & (gap <= 2 * W)).astype(np.float32).astype(jnp.bfloat16)


def lag_weights():
    order = np.concatenate([np.arange(0, F, 2), np.arange(1, F, 2)])
    shifts = np.arange(LAGS) - LAGS // 2
    c, s = cos_sin((F0 + order)[:, None] * shifts[None, :], L, 1.0 / math.sqrt(F))
    pieces = []
    for k in range(0, F, CHUNK):
        pieces += [c[k : k + CHUNK], s[k : k + CHUNK]]
    return np.concatenate(pieces, axis=0).astype(jnp.bfloat16)


def split_hi_lo(value):
    high = value.astype(jnp.bfloat16)
    low = (value - high.astype(jnp.float32)).astype(jnp.bfloat16)
    return jnp.concatenate([high, low], axis=1)


def whiten_kernel(
    x_ref, use_ref, even_hbm, odd_hbm, ones_hbm, out_ref, mark_ref, even, odd, ones, sem
):
    stations = x_ref.shape[1]
    loads = [
        pltpu.make_async_copy(src, dst, sem.at[k])
        for k, (src, dst) in enumerate(((even_hbm, even), (odd_hbm, odd), (ones_hbm, ones)))
    ]
    for load in loads:
        load.start()
    flags = use_ref[...].astype(jnp.float32)
    mark_ref[...] = jnp.broadcast_to(flags, mark_ref.shape).astype(jnp.bfloat16)
    early = x_ref[:HALF].astype(jnp.float32)
    late = x_ref[HALF:].astype(jnp.float32)

    def transform(load, table, signal):
        signal = split_hi_lo(signal)
        load.wait()
        both = jnp.dot(table[...], signal, preferred_element_type=jnp.float32)
        both = both[:, :stations] + both[:, stations:]
        return both[:HE], both[HE:]

    re_even, im_even = transform(loads[0], even, early + late)
    re_odd, im_odd = transform(loads[1], odd, early - late)
    power = jnp.concatenate(
        [re_even * re_even + im_even * im_even, re_odd * re_odd + im_odd * im_odd], axis=0
    )
    loads[2].wait()
    total = jnp.dot(ones[...], split_hi_lo(power), preferred_element_type=jnp.float32)
    smooth = (total[:, :stations] + total[:, stations:]) * jnp.float32(1.0 / (2 * W + 1))
    weight = flags / jnp.sqrt(smooth + 1e-05)
    w2 = W // 2
    for k in range(CHUNKS):
        at = k * CHUNK
        real, imag = (re_even, im_even) if at < HF else (re_odd, im_odd)
        inner = w2 + at % HF
        scale = weight[at : at + CHUNK]
        out_ref[k, :, :CHUNK] = (real[inner : inner + CHUNK] * scale).T.astype(jnp.bfloat16)
        out_ref[k, :, CHUNK:] = (imag[inner : inner + CHUNK] * scale).T.astype(jnp.bfloat16)


def exchange_kernel(
    pairs, width, hours, pair_ref, ask_ref, w_ref, f_ref, bj, bi, bf,
    *scratch,
):
    rows = w_ref.shape[1]
    part = rows // hours
    span_rows = rows // SPLIT
    units = CHUNKS * SPLIT
    g = scratch[:units]
    (
        gf, sj, si, sf, hand, hand_f, asks, zx_send, zx_recv, j_send, j_recv, relay_send,
        i_send, i_recv, f_send, f_recv, local_sem, i_local, a_send, a_recv, x_send, x_recv,
    ) = scratch[units:]
    depth = pairs // width
    p = lax.axis_index("pairs")
    me = lax.axis_index("hours")
    z, x = p // width, p % width
    y, core = me // CORES, me % CORES
    partner = y * CORES + (1 - core)
    flags_unit = units

    def place(u):
        return u // SPLIT, pl.ds((u % SPLIT) * span_rows, span_rows)

    def beside(k):
        return z * width + (x + k) % width

    steps = (
        (z + 1 < depth, p + width),
        (z > 0, p - width),
    )

    barrier = pltpu.get_barrier_semaphore()
    for exists, target in steps:
        @pl.when(exists)
        def _(target=target):
            pl.semaphore_signal(barrier, inc=1, device_id={"pairs": target}, device_id_type=MESH)
    for k in range(1, hours):
        pl.semaphore_signal(
            barrier, inc=1, device_id={"hours": (me + k) % hours}, device_id_type=MESH
        )
    for k in range(1, width):
        pl.semaphore_signal(
            barrier, inc=1, device_id={"pairs": beside(k)}, device_id_type=MESH
        )
    near = sum(e.astype(jnp.int32) for e, _ in steps)
    pl.semaphore_wait(barrier, near + hours - 1 + width - 1)

    pending = []

    def slot(b, u):
        return gf.at[b // width] if u == flags_unit else g[u].at[b // width]

    def own(u):
        return f_ref if u == flags_unit else w_ref.at[place(u)]

    def forward(cond, b, u, way, is_own=False):
        exists, target = steps[way]
        both = exists if cond is None else jnp.logical_and(cond, exists)

        def make():
            return pltpu.make_async_remote_copy(
                src_ref=own(u) if is_own else slot(b, u),
                dst_ref=slot(b, u),
                send_sem=zx_send.at[way, b // width, u],
                recv_sem=zx_recv.at[b // width, u],
                device_id={"pairs": target},
                device_id_type=MESH,
            )

        @pl.when(both)
        def _():
            make().start()
        pending.append((both, make))

    def arrived(b, u):
        pltpu.make_async_remote_copy(
            src_ref=slot(b, u), dst_ref=slot(b, u), send_sem=zx_send.at[0, b // width, u],
            recv_sem=zx_recv.at[b // width, u], device_id={"pairs": p}, device_id_type=MESH,
        ).wait_recv()

    def send_own(u):
        for way in range(4):
            forward(None, p, u, way, is_own=True)

    keep = [
        pltpu.make_async_copy(own(u), slot(p, u), local_sem.at[u]) for u in range(units + 1)
    ]
    for copy in keep:
        copy.start()

    def gather_z(u, d):
        for way, b, cond in (
            (0, p - d * width, z - d >= 0),
            (1, p + d * width, z + d < depth),
        ):
            @pl.when(cond)
            def _(b=b):
                arrived(b, u)
            forward(cond, b, u, way)

    def crossing(k, u):
        hand_of = hand_f.at[k - 1] if u == flags_unit else hand.at[k - 1, u]
        dst = gf if u == flags_unit else g[u]
        return pltpu.make_async_remote_copy(
            src_ref=hand_of,
            dst_ref=dst.at[pl.ds(depth + 2 * (width - k - 1), 2)],
            send_sem=x_send.at[k - 1, u],
            recv_sem=x_recv.at[width - k - 1, u],
            device_id={"pairs": beside(k)},
            device_id_type=MESH,
        )

    def offer(u):
        keep[u].wait()
        pool = gf if u == flags_unit else g[u]
        for k in range(1, width):
            for s in range(2):
                asked = asks[k - 1, s, 0:1, 0:1].astype(jnp.float32)
                picked = None
                for zz in range(depth):
                    mark = jnp.where(asked == (zz * width + x).astype(jnp.float32), 1.0, 0.0)
                    term = pool[zz].astype(jnp.float32) * mark
                    picked = term if picked is None else picked + term
                if u == flags_unit:
                    hand_f[k - 1, s] = picked.astype(jnp.bfloat16)
                else:
                    hand[k - 1, u, s] = picked.astype(jnp.bfloat16)
            crossing(k, u).start()

    def chosen(s):
        b = pair_ref[0, s]
        away = lax.rem(lax.rem(b, width) - x + width, width)
        return jnp.where(away == 0, b // width, depth + 2 * (away - 1) + s)

    late = []
    local = []

    def remote(src, dst, send_sem, recv_sem, target):
        copy = pltpu.make_async_remote_copy(
            src_ref=src, dst_ref=dst, send_sem=send_sem, recv_sem=recv_sem,
            device_id={"hours": target}, device_id_type=MESH,
        )
        copy.start()
        late.append(copy)

    def stay(src, dst, sem):
        copy = pltpu.make_async_copy(src, dst, sem)
        copy.start()
        local.append(copy)

    def share(u):
        for k in range(1, width):
            crossing(width - k, u).wait_recv()
        if u == flags_unit:
            sf[0] = gf[chosen(0)]
            sf[1] = gf[chosen(1)]
            for k in range(1, hours):
                remote(sf, bf.at[me], f_send.at[k], f_recv.at[me], (me + k) % hours)
            stay(sf, bf.at[me], local_sem.at[units + 1])
            return
        c, span = place(u)
        sj[u] = g[u][chosen(1)]
        si[u] = g[u][chosen(0)]
        for k in range(1, hours // CORES):
            target = ((y + k) % (hours // CORES)) * CORES + core
            remote(sj.at[u], bj.at[me, c, span], j_send.at[k, u], j_recv.at[me, u], target)
        remote(sj.at[u], bj.at[me, c, span], j_send.at[0, u], j_recv.at[me, u], partner)
        stay(sj.at[u], bj.at[me, c, span], local_sem.at[units + 2 + u])
        share_hours = hours // SPLIT
        for k in range(share_hours):
            peer = (u % SPLIT) * share_hours + k
            rows_of = si.at[u, pl.ds(k * part, part)]

            def make(peer=peer, rows_of=rows_of):
                return pltpu.make_async_remote_copy(
                    src_ref=rows_of, dst_ref=bi.at[me, c], send_sem=i_send.at[c, peer],
                    recv_sem=i_recv.at[me, c], device_id={"hours": peer}, device_id_type=MESH,
                )

            @pl.when(me != peer)
            def _(make=make):
                make().start()
            pending.append((me != peer, make))

            @pl.when(me == peer)
            def _(rows_of=rows_of):
                pltpu.make_async_copy(rows_of, bi.at[me, c], i_local.at[c]).start()

    def got(sem, ref):
        pltpu.make_async_remote_copy(
            src_ref=ref, dst_ref=ref, send_sem=sem, recv_sem=sem,
            device_id={"hours": me}, device_id_type=MESH,
        ).wait_recv()

    def relay(u):
        c, span = place(u)
        for k in range(1, hours // CORES):
            peer = ((y + k) % (hours // CORES)) * CORES + core
            piece = bj.at[peer, c, span]
            got(j_recv.at[peer, u], piece)
            remote(piece, piece, relay_send.at[k, u], j_recv.at[peer, u], partner)

    def asking(k):
        return pltpu.make_async_remote_copy(
            src_ref=ask_ref, dst_ref=asks.at[width - k - 1], send_sem=a_send.at[k - 1],
            recv_sem=a_recv.at[width - k - 1], device_id={"pairs": beside(k)},
            device_id_type=MESH,
        )

    order = [flags_unit] + list(range(units))
    for k in range(1, width):
        asking(k).start()
    for t in range(len(order) + depth + 3):
        if t < len(order):
            for way in range(2):
                forward(None, p, order[t], way, is_own=True)
        for d in range(1, depth):
            if 0 <= t - d < len(order):
                gather_z(order[t - d], d)
        if t == depth - 1:
            for k in range(1, width):
                asking(width - k).wait_recv()
        if 0 <= t - depth + 1 < len(order):
            offer(order[t - depth + 1])
        if 0 <= t - depth - 1 < len(order):
            share(order[t - depth - 1])
        if 1 <= t - depth - 2 < len(order):
            relay(order[t - depth - 2])

    for k in range(1, width):
        asking(k).wait_send()
        for u in range(units + 1):
            crossing(k, u).wait_send()
    for u in range(units):
        c, span = place(u)
        for k in range(hours // CORES):
            peer = ((y + k) % (hours // CORES)) * CORES + (1 - core)
            got(j_recv.at[peer, u], bj.at[peer, c, span])
    for k in range(1, hours):
        peer = (me + k) % hours
        for c in range(CHUNKS):
            got(i_recv.at[peer, c], bi.at[peer, c])
        got(f_recv.at[peer], bf.at[peer])
    for copy in local:
        copy.wait()
    for c in range(CHUNKS):
        pltpu.make_async_copy(bi.at[me, c], bi.at[me, c], i_local.at[c]).wait()
    for cond, make in pending:
        @pl.when(cond)
        def _(make=make):
            make().wait_send()
    for copy in late:
        copy.wait_send()


SPLIT = 2


def exchange(pair_blocks, asks, whitened, marks, pairs, width, hours):
    rows, cols = whitened.shape[1:]
    part = rows // hours
    units = CHUNKS * SPLIT
    any_space = pl.BlockSpec(memory_space=pl.ANY)
    dma = pltpu.SemaphoreType.DMA
    groups = hours // CORES
    depth = pairs // width
    slots = depth + 2 * (width - 1)
    return pl.pallas_call(
        functools.partial(exchange_kernel, pairs, width, hours),
        out_shape=(
            jax.ShapeDtypeStruct((hours, CHUNKS, rows, cols), jnp.bfloat16),
            jax.ShapeDtypeStruct((hours, CHUNKS, part, cols), jnp.bfloat16),
            jax.ShapeDtypeStruct((hours, 2) + marks.shape, jnp.bfloat16),
        ),
        in_specs=[pl.BlockSpec(memory_space=pltpu.SMEM), any_space, any_space, any_space],
        out_specs=(any_space, any_space, any_space),
        scratch_shapes=[pltpu.VMEM((slots, rows // SPLIT, cols), jnp.bfloat16)] * units + [
            pltpu.VMEM((slots,) + marks.shape, jnp.bfloat16),
            pltpu.VMEM((units, rows // SPLIT, cols), jnp.bfloat16),
            pltpu.VMEM((units, rows // SPLIT, cols), jnp.bfloat16),
            pltpu.VMEM((2,) + marks.shape, jnp.bfloat16),
            pltpu.VMEM((width - 1, units, 2, rows // SPLIT, cols), jnp.bfloat16),
            pltpu.VMEM((width - 1, 2) + marks.shape, jnp.bfloat16),
            pltpu.VMEM((width - 1,) + asks.shape, asks.dtype),
            dma((2, depth, units + 1)),
            dma((depth, units + 1)),
            dma((groups, units)),
            dma((hours, units)),
            dma((groups, units)),
            dma((CHUNKS, hours)),
            dma((hours, CHUNKS)),
            dma((hours,)),
            dma((hours,)),
            dma((2 * units + 2,)),
            dma((CHUNKS,)),
            dma((width - 1,)),
            dma((width - 1,)),
            dma((width - 1, units + 1)),
            dma((width - 1, units + 1)),
        ],
        compiler_params=pltpu.CompilerParams(
            collective_id=0, has_side_effects=True, vmem_limit_bytes=32 << 20
        ),
        name="exchange",
    )(pair_blocks, asks, whitened, marks)


GROUP = 8
SUB = 2
BLOCK = 16


def stack_kernel(
    hours, me_ref, bi_ref, bj_ref, bf_ref, g_ref, out_ref, af, heads, recip, *cross
):
    step = pl.program_id(0)
    rows = bj_ref.shape[2]
    first_rows = bi_ref.shape[2]
    f32 = jnp.float32

    @pl.when(step == 0)
    def _():
        af[...] = bi_ref[...].astype(f32)
        first = bf_ref[:, 0, 0, :]
        second = bf_ref[:, 1, 0, :]
        counts = lax.dot_general(
            second, first, (((0,), (0,)), ((), ())), preferred_element_type=f32
        )
        recip[...] = 1.0 / jnp.maximum(counts, 1.0)

    offset = me_ref[0] * first_rows + step * GROUP
    scale = pltpu.roll(recip[...], (rows - offset) % rows, 1)
    at_rows = pl.ds(pl.multiple_of(step * GROUP, GROUP), GROUP)
    for h in range(hours):
        for c in range(CHUNKS):
            ar = af[h, c, at_rows, :CHUNK]
            ai = af[h, c, at_rows, CHUNK:]
            for k, value in enumerate((ar, ai)):
                for a in range(GROUP):
                    heads[a, c, h, k] = jnp.broadcast_to(
                        value[a : a + 1], (BLOCK, CHUNK)
                    ).astype(jnp.bfloat16)

    for sub in range(GROUP // SUB):
        buf = cross[sub]
        for c in range(CHUNKS):
            lo = 2 * CHUNK * c
            hi = lo + CHUNK
            for r in range(0, rows, BLOCK):
                tails = []
                for h in range(hours):
                    tails.append(
                        (
                            bj_ref[h, c, r : r + BLOCK, :CHUNK],
                            bj_ref[h, c, r : r + BLOCK, CHUNK:],
                        )
                    )
                for a in range(SUB):
                    real = imag = None
                    for h in range(hours):
                        ar, ai = heads[sub * SUB + a, c, h, 0], heads[sub * SUB + a, c, h, 1]
                        br, bm = tails[h]
                        re = ar * br + ai * bm
                        im = ai * br - ar * bm
                        real = re if real is None else real + re
                        imag = im if imag is None else imag + im
                    at = a * rows + r
                    buf[at : at + BLOCK, lo:hi] = real
                    buf[at : at + BLOCK, hi : hi + CHUNK] = imag
        lagged = jnp.dot(buf[...], g_ref[...], preferred_element_type=f32)
        for a in range(SUB):
            k = sub * SUB + a
            out_ref[0, k] = lagged[a * rows : (a + 1) * rows] * scale[:, k : k + 1]


def stack(me, bi, bj, bf, weights):
    hours, _, first_rows, cols = bi.shape
    rows = bj.shape[2]
    full = lambda a: pl.BlockSpec(a.shape, lambda i, *_: (0,) * a.ndim, pipeline_mode=pl.Buffered(1))
    return pl.pallas_call(
        functools.partial(stack_kernel, hours),
        grid_spec=pltpu.PrefetchScalarGridSpec(
            num_scalar_prefetch=1,
            grid=(first_rows // GROUP,),
            in_specs=[full(bi), full(bj), full(bf), full(weights)],
            out_specs=pl.BlockSpec((1, GROUP, rows, LAGS), lambda i, *_: (0, i, 0, 0)),
            scratch_shapes=[
                pltpu.VMEM((hours, CHUNKS, first_rows, cols), jnp.float32),
                pltpu.VMEM((GROUP, CHUNKS, hours, 2, BLOCK, CHUNK), jnp.bfloat16),
                pltpu.VMEM((rows, rows), jnp.float32),
            ]
            + [pltpu.VMEM((SUB * rows, 2 * F), jnp.bfloat16)] * (GROUP // SUB),
        ),
        out_shape=jax.ShapeDtypeStruct((1, first_rows, rows, LAGS), jnp.float32),
        compiler_params=pltpu.CompilerParams(vmem_limit_bytes=48 << 20),
        name="stack",
    )(me, bi, bj, bf, weights)


def whiten(records, usable):
    rows = records.shape[0]
    samples = records.reshape(rows, L).T
    even, odd = spectrum_tables()
    tables = (jnp.asarray(even), jnp.asarray(odd), jnp.asarray(window_ones()))
    vmem = pl.BlockSpec(memory_space=pltpu.VMEM)
    hbm = pl.BlockSpec(memory_space=pltpu.HBM)
    return pl.pallas_call(
        whiten_kernel,
        out_shape=(
            jax.ShapeDtypeStruct((CHUNKS, rows, 2 * CHUNK), jnp.bfloat16),
            jax.ShapeDtypeStruct((16, rows), jnp.bfloat16),
        ),
        in_specs=[vmem, vmem, hbm, hbm, hbm],
        out_specs=(vmem, vmem),
        scratch_shapes=[pltpu.VMEM(t.shape, t.dtype) for t in tables]
        + [pltpu.SemaphoreType.DMA((3,))],
        compiler_params=pltpu.CompilerParams(vmem_limit_bytes=63 << 20),
        name="whiten",
    )(samples, usable.reshape(1, rows), *tables)


def solution(mesh):
    pairs, hours = mesh.shape["pairs"], mesh.shape["hours"]
    width = 1 << ((pairs.bit_length() - 1) // 2)

    def body(records, usable, pair_blocks):
        whitened, marks = whiten(records, usable)
        asks = jnp.broadcast_to(
            pair_blocks.reshape(2, 1, 1).astype(jnp.float32), (2, 8, 128)
        )
        bj, bi, bf = exchange(pair_blocks, asks, whitened, marks, pairs, width, hours)
        me = lax.axis_index("hours").astype(jnp.int32).reshape(1)
        return stack(me, bi, bj, bf, jnp.asarray(lag_weights()))

    return jax.shard_map(
        body,
        mesh=mesh,
        in_specs=(P("pairs", "hours", None), P("pairs", "hours"), P("pairs", None)),
        out_specs=P("pairs", "hours", None, None),
        check_vma=False,
    )
```

profile of v0, /device:TPU:1, one launch (start us, length us, event | category | flops | bytes accessed | tf_op | source)
XLA Modules:
  0.0 61.4 jit_solution(14135182195470029484)
XLA Ops:
  0.0 0.7 %convert_bitcast_fusion = f32[2]{0:T(128)S(1)} fusion(s32[1,2]{1,0:T(1,128)} %pair_ref.1), kind=kLoop, calls=%fused_computation | loop fusion | flops 2 | bytes 16 | tf_op jit(solution)/shard_map/convert_element_type | solution.py:537
  0.7 0.1 broadcast_in_dim.2.ask_ref
  0.7 0.0 copy-start.3
  0.7 0.0 copy-start
  0.7 6.9 %whiten.1 = (bf16[4,128,256]{2,1,0:T(8,128)(2,1)}, bf16[16,128]{1,0:T(8,128)(2,1)}) custom-call(bf16[3600,128]{1,0:T(8,128)(2,1)} %bitcast.7, s32[1,128]{1,0:T(1,128)} %bitcast.8, bf16[576,1800]{1,0:T(8,128)(2,1)} %constant.12.clone.even_hbm, bf16[576,1800]{1,0:T(8,128)(2,1)} %constant.13.clone.odd_hbm, bf16[512,576]{1,0:T(8,128)(2,1)} %constant.14.clone.ones_hbm), custom_call_target="tpu_custom_call" | custom-call | tf_op jit(solution)/shard_map/whiten/pallas_call | solution.py:515
  7.7 0.0 copy-done.3
  7.7 0.0 copy-start.1
  7.7 0.9 %copy-done.1 = bf16[4,128,256]{2,1,0:T(8,128)(2,1)S(1)} copy-done((bf16[4,128,256]{2,1,0:T(8,128)(2,1)S(1)}, bf16[4,128,256]{2,1,0:T(8,128)(2,1)}, u32[]{:S(2)}) %copy-start.1) | copy-done | bytes 262168
  8.7 0.0 copy-start.2
  8.7 0.7 %copy-done.2 = bf16[16,128]{1,0:T(8,128)(2,1)S(1)} copy-done((bf16[16,128]{1,0:T(8,128)(2,1)S(1)}, bf16[16,128]{1,0:T(8,128)(2,1)}, u32[]{:S(2)}) %copy-start.2) | copy-done | bytes 4120
  9.3 41.3 %exchange.1 = (bf16[4,4,128,256]{3,2,1,0:T(8,128)(2,1)S(1)}, bf16[4,4,32,256]{3,2,1,0:T(8,128)(2,1)S(1)}, bf16[4,2,16,128]{3,2,1,0:T(8,128)(2,1)S(1)}) custom-call(s32[1,2]{1,0:T(1,128)S(1)} %copy-done.3, f32[2,8,128]{2,1,0:T(8,128)S(1)} %broadcast_in_dim.2.ask_ref, bf16[4,128,256]{2,1,0:T(8,128)(2,1)S(1)} %copy-done.1, bf16[16,128]{1,0:T(8,128)(2,1)S(1)} %copy-done.2), custom_call_target="tpu_custom_call" | custom-call | tf_op jit(solution)/shard_map/exchange/pallas_call | solution.py:376
  50.7 0.0 copy-done
  50.7 10.7 %stack.1 = f32[1,32,128,256]{3,2,1,0:T(8,128)} custom-call(s32[1]{0:T(128)} %bitcast.me_ref, bf16[4,4,32,256]{3,2,1,0:T(8,128)(2,1)S(1)} %get-tuple-element.12.bi_ref, bf16[4,4,128,256]{3,2,1,0:T(8,128)(2,1)S(1)} %get-tuple-element.13.bj_ref, bf16[4,2,16,128]{3,2,1,0:T(8,128)(2,1)S(1)} %get-tuple-element.14.bf_ref, bf16[1024,256]{1,0:T(8,128)(2,1)S(1)} %copy-done), custom_call_target="tpu_custom_call" | custom-call | tf_op jit(solution)/shard_map/stack/pallas_call | solution.py:488
Async XLA Ops:
  0.7 7.0 %copy-start.3 = (s32[1,2]{1,0:T(1,128)S(1)}, s32[1,2]{1,0:T(1,128)}, u32[]{:S(2)}) copy-start(s32[1,2]{1,0:T(1,128)} %pair_ref.1) | copy-start | bytes 28
  0.7 49.9 %copy-start = (bf16[1024,256]{1,0:T(8,128)(2,1)S(1)}, bf16[1024,256]{1,0:T(8,128)(2,1)}, u32[]{:S(2)}) copy-start(bf16[1024,256]{1,0:T(8,128)(2,1)} %constant.15.clone.g_ref) | copy-start | bytes 1572868
  7.7 1.0 %copy-start.1 = (bf16[4,128,256]{2,1,0:T(8,128)(2,1)S(1)}, bf16[4,128,256]{2,1,0:T(8,128)(2,1)}, u32[]{:S(2)}) copy-start(bf16[4,128,256]{2,1,0:T(8,128)(2,1)} %get-tuple-element.10.w_ref) | copy-start | bytes 786436
  8.7 0.7 %copy-start.2 = (bf16[16,128]{1,0:T(8,128)(2,1)S(1)}, bf16[16,128]{1,0:T(8,128)(2,1)}, u32[]{:S(2)}) copy-start(bf16[16,128]{1,0:T(8,128)(2,1)} %get-tuple-element.11.f_ref) | copy-start | bytes 12292
where the time goes:
time: 61.6 us; the launch traced here: 61.4 us
  Pallas kernels  59 us (96%)
  local copies, waits for them, and re-layouts  1.71 us (3%)
  other arithmetic  0.66 us (1%)
    pallas_call x1, Pallas kernels, exchange(): pl.pallas_call(functools.partial(exchange_kernel, pairs, width, hours), o...  41.3 us
    pallas_call x1, Pallas kernels, stack(): pl.pallas_call(functools.partial(stack_kernel, hours), grid_spec=pltpu.Pr...  10.7 us
    pallas_call x1, Pallas kernels, whiten(): pl.pallas_call(whiten_kernel, out_shape=(jax.ShapeDtypeStruct((CHUNKS, ro...  6.94 us
    unnamed x8, local copies, waits for them, and re-layouts  1.64 us

commit v1 on v0

--- a/solution.py
+++ b/solution.py
@@ -29,7 +29,7 @@
     return np.cos(wide).astype(np.float32) * scale, -np.sin(wide).astype(np.float32) * scale
 
 
-CHUNK = 128
+CHUNK = 256
 CHUNKS = F // CHUNK
 
 
@@ -361,7 +361,7 @@
         copy.wait_send()
 
 
-SPLIT = 2
+SPLIT = 4
 
 
 def exchange(pair_blocks, asks, whitened, marks, pairs, width, hours):
@@ -415,7 +415,7 @@
 
 GROUP = 8
 SUB = 2
-BLOCK = 16
+BLOCK = 8
 
 
 def stack_kernel(

time: 61.6 us -> 57.3 us (0.930)
  Pallas kernels: 59 us -> 54.7 us
    pallas_call x1, Pallas kernels: 10.7 us -> 6.37 us  [stack(): pl.pallas_call(functools.partial(stack_kernel, hours), grid_spec=pltpu.Pr...]
where the time goes in v1:
time: 57.3 us; the launch traced here: 57.1 us
  Pallas kernels  54.7 us (95%)
  local copies, waits for them, and re-layouts  1.71 us (3%)
  other arithmetic  0.66 us (1%)
    pallas_call x1, Pallas kernels, exchange(): pl.pallas_call(functools.partial(exchange_kernel, pairs, width, hours), o...  41.4 us
    pallas_call x1, Pallas kernels, whiten(): pl.pallas_call(whiten_kernel, out_shape=(jax.ShapeDtypeStruct((CHUNKS, ro...  6.94 us
    pallas_call x1, Pallas kernels, stack(): pl.pallas_call(functools.partial(stack_kernel, hours), grid_spec=pltpu.Pr...  6.37 us
    unnamed x8, local copies, waits for them, and re-layouts  1.64 us

profile of v1, /device:TPU:1, one launch (start us, length us, event | category | flops | bytes accessed | tf_op | source)
XLA Modules:
  0.0 57.1 jit_solution(15304576339165227681)
XLA Ops:
  0.0 0.7 %convert_bitcast_fusion = f32[2]{0:T(128)S(1)} fusion(s32[1,2]{1,0:T(1,128)} %pair_ref.1), kind=kLoop, calls=%fused_computation | loop fusion | flops 2 | bytes 16 | tf_op jit(solution)/shard_map/convert_element_type | solution.py:537
  0.7 0.1 broadcast_in_dim.2.ask_ref
  0.7 0.0 copy-start.3
  0.7 0.0 copy-start
  0.7 6.9 %whiten.1 = (bf16[2,128,512]{2,1,0:T(8,128)(2,1)}, bf16[16,128]{1,0:T(8,128)(2,1)}) custom-call(bf16[3600,128]{1,0:T(8,128)(2,1)} %bitcast.7, s32[1,128]{1,0:T(1,128)} %bitcast.8, bf16[576,1800]{1,0:T(8,128)(2,1)} %constant.12.clone.even_hbm, bf16[576,1800]{1,0:T(8,128)(2,1)} %constant.13.clone.odd_hbm, bf16[512,576]{1,0:T(8,128)(2,1)} %constant.14.clone.ones_hbm), custom_call_target="tpu_custom_call" | custom-call | tf_op jit(solution)/shard_map/whiten/pallas_call | solution.py:515
  7.7 0.0 copy-done.3
  7.7 0.0 copy-start.1
  7.7 0.9 %copy-done.1 = bf16[2,128,512]{2,1,0:T(8,128)(2,1)S(1)} copy-done((bf16[2,128,512]{2,1,0:T(8,128)(2,1)S(1)}, bf16[2,128,512]{2,1,0:T(8,128)(2,1)}, u32[]{:S(2)}) %copy-start.1) | copy-done | bytes 262168
  8.7 0.0 copy-start.2
  8.7 0.7 %copy-done.2 = bf16[16,128]{1,0:T(8,128)(2,1)S(1)} copy-done((bf16[16,128]{1,0:T(8,128)(2,1)S(1)}, bf16[16,128]{1,0:T(8,128)(2,1)}, u32[]{:S(2)}) %copy-start.2) | copy-done | bytes 4120
  9.3 41.4 %exchange.1 = (bf16[4,2,128,512]{3,2,1,0:T(8,128)(2,1)S(1)}, bf16[4,2,32,512]{3,2,1,0:T(8,128)(2,1)S(1)}, bf16[4,2,16,128]{3,2,1,0:T(8,128)(2,1)S(1)}) custom-call(s32[1,2]{1,0:T(1,128)S(1)} %copy-done.3, f32[2,8,128]{2,1,0:T(8,128)S(1)} %broadcast_in_dim.2.ask_ref, bf16[2,128,512]{2,1,0:T(8,128)(2,1)S(1)} %copy-done.1, bf16[16,128]{1,0:T(8,128)(2,1)S(1)} %copy-done.2), custom_call_target="tpu_custom_call" | custom-call | tf_op jit(solution)/shard_map/exchange/pallas_call | solution.py:376
  50.7 0.0 copy-done
  50.7 6.4 %stack.1 = f32[1,32,128,256]{3,2,1,0:T(8,128)} custom-call(s32[1]{0:T(128)} %bitcast.me_ref, bf16[4,2,32,512]{3,2,1,0:T(8,128)(2,1)S(1)} %get-tuple-element.12.bi_ref, bf16[4,2,128,512]{3,2,1,0:T(8,128)(2,1)S(1)} %get-tuple-element.13.bj_ref, bf16[4,2,16,128]{3,2,1,0:T(8,128)(2,1)S(1)} %get-tuple-element.14.bf_ref, bf16[1024,256]{1,0:T(8,128)(2,1)S(1)} %copy-done), custom_call_target="tpu_custom_call" | custom-call | tf_op jit(solution)/shard_map/stack/pallas_call | solution.py:488
Async XLA Ops:
  0.7 7.0 %copy-start.3 = (s32[1,2]{1,0:T(1,128)S(1)}, s32[1,2]{1,0:T(1,128)}, u32[]{:S(2)}) copy-start(s32[1,2]{1,0:T(1,128)} %pair_ref.1) | copy-start | bytes 28
  0.7 50.0 %copy-start = (bf16[1024,256]{1,0:T(8,128)(2,1)S(1)}, bf16[1024,256]{1,0:T(8,128)(2,1)}, u32[]{:S(2)}) copy-start(bf16[1024,256]{1,0:T(8,128)(2,1)} %constant.15.clone.g_ref) | copy-start | bytes 1572868
  7.7 1.0 %copy-start.1 = (bf16[2,128,512]{2,1,0:T(8,128)(2,1)S(1)}, bf16[2,128,512]{2,1,0:T(8,128)(2,1)}, u32[]{:S(2)}) copy-start(bf16[2,128,512]{2,1,0:T(8,128)(2,1)} %get-tuple-element.10.w_ref) | copy-start | bytes 786436
  8.7 0.7 %copy-start.2 = (bf16[16,128]{1,0:T(8,128)(2,1)S(1)}, bf16[16,128]{1,0:T(8,128)(2,1)}, u32[]{:S(2)}) copy-start(bf16[16,128]{1,0:T(8,128)(2,1)} %get-tuple-element.11.f_ref) | copy-start | bytes 12292

commit v2 on v1

v2 whole, which is shorter than its diff:
```python
import functools
import math

import jax
import jax.numpy as jnp
import numpy as np
from jax import lax
from jax.experimental import pallas as pl
from jax.experimental.pallas import tpu as pltpu
from jax.sharding import PartitionSpec as P

L = 3600
F = 512
W = 32
F0 = 64
LAGS = 256
EXTENT = F + 2 * W
HALF = L // 2
HE = EXTENT // 2
HF = F // 2
CORES = 2
MESH = pl.DeviceIdType.MESH


def cos_sin(phases, length, scale):
    angles = np.float32(2.0 * math.pi / length) * (phases % length).astype(np.float32)
    wide = angles.astype(np.float64)
    scale = np.float32(scale)
    return np.cos(wide).astype(np.float32) * scale, -np.sin(wide).astype(np.float32) * scale


CHUNK = 256
CHUNKS = F // CHUNK


def spectrum_tables():
    bins = F0 - W + np.arange(EXTENT)
    c, q = cos_sin(bins[:, None] * np.arange(HALF)[None, :], L, 1.0 / math.sqrt(L))
    even = np.concatenate([c[0::2], q[0::2]], axis=0)
    odd = np.concatenate([c[1::2], q[1::2]], axis=0)
    return even.astype(jnp.bfloat16), odd.astype(jnp.bfloat16)


def window_ones():
    source = np.concatenate([np.arange(0, EXTENT, 2), np.arange(1, EXTENT, 2)])
    target = np.concatenate([np.arange(0, F, 2), np.arange(1, F, 2)])
    gap = source[None, :] - target[:, None]
    return ((gap >= 0) & (gap <= 2 * W)).astype(np.float32).astype(jnp.bfloat16)


def lag_weights():
    order = np.concatenate([np.arange(0, F, 2), np.arange(1, F, 2)])
    shifts = np.arange(LAGS) - LAGS // 2
    c, s = cos_sin((F0 + order)[:, None] * shifts[None, :], L, 1.0 / math.sqrt(F))
    pieces = []
    for k in range(0, F, CHUNK):
        pieces += [c[k : k + CHUNK], s[k : k + CHUNK]]
    return np.concatenate(pieces, axis=0).astype(jnp.bfloat16)


def split_hi_lo(value):
    high = value.astype(jnp.bfloat16)
    low = (value - high.astype(jnp.float32)).astype(jnp.bfloat16)
    return jnp.concatenate([high, low], axis=1)


def whiten_kernel(
    x_ref, use_ref, even_hbm, odd_hbm, ones_hbm, out_ref, even, odd, ones, sem
):
    stations = x_ref.shape[1]
    loads = [
        pltpu.make_async_copy(src, dst, sem.at[k])
        for k, (src, dst) in enumerate(((even_hbm, even), (odd_hbm, odd), (ones_hbm, ones)))
    ]
    for load in loads:
        load.start()
    flags = use_ref[...].astype(jnp.float32)
    early = x_ref[:HALF].astype(jnp.float32)
    late = x_ref[HALF:].astype(jnp.float32)

    def transform(load, table, signal):
        signal = split_hi_lo(signal)
        load.wait()
        both = jnp.dot(table[...], signal, preferred_element_type=jnp.float32)
        both = both[:, :stations] + both[:, stations:]
        return both[:HE], both[HE:]

    re_even, im_even = transform(loads[0], even, early + late)
    re_odd, im_odd = transform(loads[1], odd, early - late)
    power = jnp.concatenate(
        [re_even * re_even + im_even * im_even, re_odd * re_odd + im_odd * im_odd], axis=0
    )
    loads[2].wait()
    total = jnp.dot(ones[...], split_hi_lo(power), preferred_element_type=jnp.float32)
    smooth = (total[:, :stations] + total[:, stations:]) * jnp.float32(1.0 / (2 * W + 1))
    weight = flags / jnp.sqrt(smooth + 1e-05)
    w2 = W // 2
    for k in range(CHUNKS):
        at = k * CHUNK
        real, imag = (re_even, im_even) if at < HF else (re_odd, im_odd)
        inner = w2 + at % HF
        scale = weight[at : at + CHUNK]
        out_ref[k, :, :CHUNK] = (real[inner : inner + CHUNK] * scale).T.astype(jnp.bfloat16)
        out_ref[k, :, CHUNK:] = (imag[inner : inner + CHUNK] * scale).T.astype(jnp.bfloat16)


UNIT = 16
LAG = 1.6


def exchange_kernel(pairs, width, hours, pair_ref, use_ref, w_ref, bj, bi, ff, *scratch):
    rows = w_ref.shape[1]
    depth = pairs // width
    groups = hours // CORES
    part = rows // width
    peer_rows = rows // hours
    pieces = part // UNIT
    subs = peer_rows // UNIT
    units = CHUNKS * pieces
    base = depth * width
    pools, sels, picks = scratch[:units], scratch[units : 2 * units], scratch[2 * units : 3 * units]
    (
        asks, far, keep_sem, stay_sem, ask_send, ask_recv, far_send, far_recv,
        fh_send, fh_recv, fx_send, fx_recv, fz_send, fz_recv, f_local,
        cross_send, cross_recv, z_send, z_recv, sel_send, sel_recv, pick_send, pick_recv,
        i_send, i_recv, i_local, j_send, j_recv, relay_send,
    ) = scratch[3 * units :]
    p = lax.axis_index("pairs")
    me = lax.axis_index("hours")
    z, x = p // width, p % width
    y, core = me // CORES, me % CORES
    partner = y * CORES + (1 - core)
    middle = jnp.logical_and(z > 0, z < depth - 1)

    def beside(k):
        return (x + k + width) % width

    def span(u, at):
        c, q = u // pieces, u % pieces
        return c, pl.ds(pl.multiple_of(at * part + q * UNIT, UNIT), UNIT)

    barrier = pltpu.get_barrier_semaphore()
    for k in range(width):
        for h in range(hours):
            if k == 0 and h == 0:
                continue
            pl.semaphore_signal(
                barrier, inc=1,
                device_id={"pairs": z * width + beside(k), "hours": (me + h) % hours},
                device_id_type=MESH,
            )
    for k in range(1, depth):
        pl.semaphore_signal(
            barrier, inc=1, device_id={"pairs": ((z + k) % depth) * width + x},
            device_id_type=MESH,
        )
    pl.semaphore_wait(barrier, width * hours - 1 + depth - 1)

    pending = []

    def send(src, dst, send_sem, recv_sem, device_id, cond=None):
        def make():
            return pltpu.make_async_remote_copy(
                src_ref=src, dst_ref=dst, send_sem=send_sem, recv_sem=recv_sem,
                device_id=device_id, device_id_type=MESH,
            )

        if cond is None:
            make().start()
        else:
            @pl.when(cond)
            def _():
                make().start()
        pending.append((cond, make))

    def got(ref, sem):
        pltpu.make_async_remote_copy(
            src_ref=ref, dst_ref=ref, send_sem=sem, recv_sem=sem,
            device_id={"hours": me}, device_id_type=MESH,
        ).wait_recv()

    def stay(src, dst, sem):
        copy = pltpu.make_async_copy(src, dst, sem)
        copy.start()
        return copy

    for s in range(2):
        asks[x, 0, s] = pair_ref[0, s]
    for k in range(1, width):
        send(
            pair_ref, asks.at[x], ask_send.at[k], ask_recv.at[x],
            {"pairs": z * width + beside(k)},
        )
    own_flags = stay(use_ref, ff.at[p, me], f_local)
    for h in range(1, hours):
        send(
            use_ref, ff.at[p, me], fh_send.at[h], fh_recv.at[me], {"hours": (me + h) % hours}
        )
    keep = []
    for u in range(units):
        for k in range(1, width):
            send(
                w_ref.at[span(u, beside(k))], pools[u].at[p], cross_send.at[k, u],
                cross_recv.at[k, u], {"pairs": z * width + beside(k)},
            )
        keep.append(stay(w_ref.at[span(u, x)], pools[u].at[p], keep_sem.at[u]))

    def row_of(u, r):
        return pools[u].at[pl.ds(r * width, width)]

    def carry(u, r, way, cond):
        send(
            row_of(u, r), row_of(u, r), z_send.at[way, r, u], z_recv.at[r, u],
            {"pairs": p + (width if way == 0 else -width)}, cond,
        )

    def learn(_):
        for k in range(1, width):
            got(asks.at[beside(k)], ask_recv.at[beside(k)])
        send(asks, far.at[1], far_send.at[0], far_recv.at[1], {"pairs": p + width}, z == 0)
        send(asks, far.at[0], far_send.at[1], far_recv.at[0], {"pairs": p - width}, z == depth - 1)

    def flags_row(_):
        own_flags.wait()
        for h in range(1, hours):
            peer = (me + h) % hours
            got(ff.at[p, peer], fh_recv.at[peer])
        for k in range(1, width):
            send(
                ff.at[p], ff.at[p], fx_send.at[k], fx_recv.at[x],
                {"pairs": z * width + beside(k)},
            )

    def flags_column(_):
        for k in range(1, width):
            got(ff.at[z * width + beside(k)], fx_recv.at[beside(k)])
        mine = ff.at[pl.ds(z * width, width)]
        for k in range(1, depth):
            send(
                mine, mine, fz_send.at[k], fz_recv.at[z],
                {"pairs": ((z + k) % depth) * width + x},
            )

    def know(_):
        for way, at in ((0, depth - 2), (1, 1)):
            @pl.when(z == at)
            def _(way=way):
                got(far.at[way], far_recv.at[way])

    def own_row(u):
        keep[u].wait()
        for k in range(1, width):
            got(pools[u].at[z * width + beside(-k)], cross_recv.at[k, u])
        carry(u, z, 0, z < depth - 2)
        carry(u, z, 1, z > 1)

    def near_row(d, u):
        for way, r, here, on in (
            (0, z - d, jnp.logical_and(z - d >= 0, z < depth - 1), z < depth - 2),
            (1, z + d, jnp.logical_and(z + d < depth, z > 0), z > 1),
        ):
            @pl.when(here)
            def _(r=r):
                got(row_of(u, r), z_recv.at[r, u])
            carry(u, r, way, jnp.logical_and(here, on))
        if d == depth - 2:
            for way, at in ((0, depth - 2), (1, 1)):
                @pl.when(z == at)
                def _(way=way):
                    for x2 in range(width):
                        for s in range(2):
                            sels[u][way, 2 * x2 + s] = pools[u][far[way, x2, 0, s]]
                send(
                    sels[u].at[way], pools[u].at[pl.ds(base, 2 * width)], sel_send.at[way, u],
                    sel_recv.at[u], {"pairs": p + (width if way == 0 else -width)}, z == at,
                )

    def pick(u):
        @pl.when(jnp.logical_not(middle))
        def _():
            got(pools[u].at[pl.ds(base, 2 * width)], sel_recv.at[u])
        c, mine = span(u, x)
        q = u % pieces
        for k in range(width):
            x2 = beside(-k)
            for s in range(2):
                b = asks[x2, 0, s]
                away = jnp.logical_and(jnp.logical_not(middle), lax.div(b, width) != z)
                picks[u][k, s] = pools[u][jnp.where(away, base + 2 * x2 + s, b)]
        for k in range(1, width):
            send(
                picks[u].at[k, 1], bj.at[me, c, mine], pick_send.at[k, u], pick_recv.at[k, u],
                {"pairs": z * width + beside(-k)},
            )
        share(u, 0, picks[u].at[0, 1])
        peer = x * (part // peer_rows) + q * UNIT // peer_rows
        sub = (q * UNIT % peer_rows) // UNIT
        land = bi.at[me, c, pl.ds(sub * UNIT, UNIT)]
        for k in range(width):
            send(
                picks[u].at[k, 0], land, i_send.at[k, u], i_recv.at[me, c, sub],
                {"pairs": z * width + beside(-k), "hours": peer}, None if k else me != peer,
            )

        @pl.when(me == peer)
        def _():
            stay(picks[u].at[0, 0], land, i_local.at[c, sub])
        stays.append(stay(picks[u].at[0, 1], bj.at[me, c, mine], stay_sem.at[u]))

    stays = []

    def share(u, k, src):
        c, at = span(u, beside(k))
        for g in range(1, groups):
            send(
                src, bj.at[me, c, at], j_send.at[g, k, u], j_recv.at[me, k, u],
                {"hours": ((y + g) % groups) * CORES + core},
            )
        send(src, bj.at[me, c, at], j_send.at[0, k, u], j_recv.at[me, k, u], {"hours": partner})

    def share_row(u):
        for k in range(1, width):
            c, at = span(u, beside(k))
            got(bj.at[me, c, at], pick_recv.at[k, u])
            share(u, k, bj.at[me, c, at])

    def relay(u):
        for k in range(width):
            c, at = span(u, beside(k))
            for g in range(1, groups):
                peer = ((y + g) % groups) * CORES + core
                piece = bj.at[peer, c, at]
                got(piece, j_recv.at[peer, k, u])
                send(
                    piece, piece, relay_send.at[g, k, u], j_recv.at[peer, k, u],
                    {"hours": partner},
                )

    steps = [(0.0, learn, 0), (LAG + 0.1, flags_row, 0), (2 * LAG + 0.1, flags_column, 0)]
    steps.append((2 * LAG + 0.2, know, 0))
    stages = [own_row]
    stages += [functools.partial(near_row, d) for d in range(1, depth - 1)]
    stages += [pick, share_row, relay]
    for n, stage in enumerate(stages):
        for u in range(units):
            steps.append(((n + 1) * LAG + u, stage, u))
    for _, stage, u in sorted(steps, key=lambda step: step[0]):
        stage(u)

    for u in range(units):
        for k in range(width):
            c, at = span(u, beside(k))
            for g in range(groups):
                peer = ((y + g) % groups) * CORES + (1 - core)
                got(bj.at[peer, c, at], j_recv.at[peer, k, u])
    near = x == me // (part // peer_rows)
    for h in range(hours):
        hour = (me + h) % hours
        for c in range(CHUNKS):
            for sub in range(subs):
                land = bi.at[hour, c, pl.ds(sub * UNIT, UNIT)]
                if h:
                    got(land, i_recv.at[hour, c, sub])
                    continue

                @pl.when(jnp.logical_not(near))
                def _(land=land, c=c, sub=sub):
                    got(land, i_recv.at[me, c, sub])

                @pl.when(near)
                def _(land=land, c=c, sub=sub):
                    pltpu.make_async_copy(land, land, i_local.at[c, sub]).wait()
    for k in range(1, depth):
        r = (z + k) % depth
        got(ff.at[pl.ds(r * width, width)], fz_recv.at[r])
    for copy in stays:
        copy.wait()
    for cond, make in pending:
        if cond is None:
            make().wait_send()
        else:
            @pl.when(cond)
            def _(make=make):
                make().wait_send()


def exchange(pair_blocks, flags, whitened, pairs, width, hours):
    rows, cols = whitened.shape[1:]
    part = rows // hours
    units = CHUNKS * (rows // width // UNIT)
    any_space = pl.BlockSpec(memory_space=pl.ANY)
    smem = pl.BlockSpec(memory_space=pltpu.SMEM)
    dma = pltpu.SemaphoreType.DMA
    groups = hours // CORES
    depth = pairs // width
    bf16 = jnp.bfloat16
    return pl.pallas_call(
        functools.partial(exchange_kernel, pairs, width, hours),
        out_shape=(
            jax.ShapeDtypeStruct((hours, CHUNKS, rows, cols), bf16),
            jax.ShapeDtypeStruct((hours, CHUNKS, part, cols), bf16),
            jax.ShapeDtypeStruct((pairs, hours) + flags.shape, flags.dtype),
        ),
        in_specs=[smem, any_space, any_space],
        out_specs=(any_space, any_space, any_space),
        scratch_shapes=[pltpu.VMEM((depth * width + 2 * width, UNIT, cols), bf16)] * units
        + [pltpu.VMEM((2, 2 * width, UNIT, cols), bf16)] * units
        + [pltpu.VMEM((width, 2, UNIT, cols), bf16)] * units
        + [
            pltpu.SMEM((width, 1, 2), jnp.int32),
            pltpu.SMEM((2, width, 1, 2), jnp.int32),
            dma((units,)),
            dma((units,)),
            dma((width,)),
            dma((width,)),
            dma((2,)),
            dma((2,)),
            dma((hours,)),
            dma((hours,)),
            dma((width,)),
            dma((width,)),
            dma((depth,)),
            dma((depth,)),
            dma(()),
            dma((width, units)),
            dma((width, units)),
            dma((2, depth, units)),
            dma((depth, units)),
            dma((2, units)),
            dma((units,)),
            dma((width, units)),
            dma((width, units)),
            dma((width, units)),
            dma((hours, CHUNKS, part // UNIT)),
            dma((CHUNKS, part // UNIT)),
            dma((groups, width, units)),
            dma((hours, width, units)),
            dma((groups, width, units)),
        ],
        compiler_params=pltpu.CompilerParams(
            collective_id=0, has_side_effects=True, vmem_limit_bytes=32 << 20
        ),
        name="exchange",
    )(pair_blocks, flags, whitened)


GROUP = 8
SUB = 2
BLOCK = 8


def stack_kernel(
    hours, me_ref, pair_ref, bi_ref, bj_ref, ff_ref, g_ref, out_ref, af, heads, recip, *cross
):
    step = pl.program_id(0)
    rows = bj_ref.shape[2]
    first_rows = bi_ref.shape[2]
    f32 = jnp.float32

    @pl.when(step == 0)
    def _():
        af[...] = bi_ref[...].astype(f32)
        first = ff_ref[pair_ref[0, 0], :, 0, :].astype(f32)
        second = ff_ref[pair_ref[0, 1], :, 0, :].astype(f32)
        counts = lax.dot_general(
            second, first, (((0,), (0,)), ((), ())), preferred_element_type=f32
        )
        recip[...] = 1.0 / jnp.maximum(counts, 1.0)

    offset = me_ref[0] * first_rows + step * GROUP
    scale = pltpu.roll(recip[...], (rows - offset) % rows, 1)
    at_rows = pl.ds(pl.multiple_of(step * GROUP, GROUP), GROUP)
    for h in range(hours):
        for c in range(CHUNKS):
            ar = af[h, c, at_rows, :CHUNK]
            ai = af[h, c, at_rows, CHUNK:]
            for k, value in enumerate((ar, ai)):
                for a in range(GROUP):
                    heads[a, c, h, k] = jnp.broadcast_to(
                        value[a : a + 1], (BLOCK, CHUNK)
                    ).astype(jnp.bfloat16)

    for sub in range(GROUP // SUB):
        buf = cross[sub]
        for c in range(CHUNKS):
            lo = 2 * CHUNK * c
            hi = lo + CHUNK
            for r in range(0, rows, BLOCK):
                tails = []
                for h in range(hours):
                    tails.append(
                        (
                            bj_ref[h, c, r : r + BLOCK, :CHUNK],
                            bj_ref[h, c, r : r + BLOCK, CHUNK:],
                        )
                    )
                for a in range(SUB):
                    real = imag = None
                    for h in range(hours):
                        ar, ai = heads[sub * SUB + a, c, h, 0], heads[sub * SUB + a, c, h, 1]
                        br, bm = tails[h]
                        re = ar * br + ai * bm
                        im = ai * br - ar * bm
                        real = re if real is None else real + re
                        imag = im if imag is None else imag + im
                    at = a * rows + r
                    buf[at : at + BLOCK, lo:hi] = real
                    buf[at : at + BLOCK, hi : hi + CHUNK] = imag
        lagged = jnp.dot(buf[...], g_ref[...], preferred_element_type=f32)
        for a in range(SUB):
            k = sub * SUB + a
            out_ref[0, k] = lagged[a * rows : (a + 1) * rows] * scale[:, k : k + 1]


def stack(me, pair_blocks, bi, bj, ff, weights):
    hours, _, first_rows, cols = bi.shape
    rows = bj.shape[2]
    full = lambda a: pl.BlockSpec(a.shape, lambda i, *_: (0,) * a.ndim, pipeline_mode=pl.Buffered(1))
    return pl.pallas_call(
        functools.partial(stack_kernel, hours),
        grid_spec=pltpu.PrefetchScalarGridSpec(
            num_scalar_prefetch=2,
            grid=(first_rows // GROUP,),
            in_specs=[full(bi), full(bj), full(ff), full(weights)],
            out_specs=pl.BlockSpec((1, GROUP, rows, LAGS), lambda i, *_: (0, i, 0, 0)),
            scratch_shapes=[
                pltpu.VMEM((hours, CHUNKS, first_rows, cols), jnp.float32),
                pltpu.VMEM((GROUP, CHUNKS, hours, 2, BLOCK, CHUNK), jnp.bfloat16),
                pltpu.VMEM((rows, rows), jnp.float32),
            ]
            + [pltpu.VMEM((SUB * rows, 2 * F), jnp.bfloat16)] * (GROUP // SUB),
        ),
        out_shape=jax.ShapeDtypeStruct((1, first_rows, rows, LAGS), jnp.float32),
        compiler_params=pltpu.CompilerParams(vmem_limit_bytes=48 << 20),
        name="stack",
    )(me, pair_blocks, bi, bj, ff, weights)


def whiten(records, usable):
    rows = records.shape[0]
    samples = records.reshape(rows, L).T
    even, odd = spectrum_tables()
    tables = (jnp.asarray(even), jnp.asarray(odd), jnp.asarray(window_ones()))
    vmem = pl.BlockSpec(memory_space=pltpu.VMEM)
    hbm = pl.BlockSpec(memory_space=pltpu.HBM)
    return pl.pallas_call(
        whiten_kernel,
        out_shape=jax.ShapeDtypeStruct((CHUNKS, rows, 2 * CHUNK), jnp.bfloat16),
        in_specs=[vmem, vmem, hbm, hbm, hbm],
        out_specs=vmem,
        scratch_shapes=[pltpu.VMEM(t.shape, t.dtype) for t in tables]
        + [pltpu.SemaphoreType.DMA((3,))],
        compiler_params=pltpu.CompilerParams(vmem_limit_bytes=63 << 20),
        name="whiten",
    )(samples, usable.reshape(1, rows), *tables)


def solution(mesh):
    pairs, hours = mesh.shape["pairs"], mesh.shape["hours"]
    width = 1 << ((pairs.bit_length() - 1) // 2)

    def body(records, usable, pair_blocks):
        whitened = whiten(records, usable)
        flags = usable.reshape(1, usable.shape[0])
        bj, bi, ff = exchange(pair_blocks, flags, whitened, pairs, width, hours)
        me = lax.axis_index("hours").astype(jnp.int32).reshape(1)
        return stack(me, pair_blocks, bi, bj, ff, jnp.asarray(lag_weights()))

    return jax.shard_map(
        body,
        mesh=mesh,
        in_specs=(P("pairs", "hours", None), P("pairs", "hours"), P("pairs", None)),
        out_specs=P("pairs", "hours", None, None),
        check_vma=False,
    )
```

time: 57.3 us -> 56.5 us (0.986)
  local copies, waits for them, and re-layouts: 1.71 us -> 0.96 us
  other arithmetic: 0.66 us -> 0 us
  Pallas kernels: 54.7 us -> 55.3 us
    pallas_call x1, Pallas kernels: 6.37 us -> 7.21 us  [stack(): pl.pallas_call(functools.partial(stack_kernel, hours), grid_spec=pltpu.Pr...]
    unnamed x8, local copies, waits for them, and re-layouts: 1.64 us -> 0.96 us
    convert_element_type x1 -> x0, other arithmetic: 0.66 us -> none  [body(): pair_blocks.reshape(2, 1, 1).astype(jnp.float32)]
where the time goes in v2:
time: 56.5 us; the launch traced here: 56.3 us
  Pallas kernels  55.3 us (98%)
  local copies, waits for them, and re-layouts  0.96 us (2%)
    pallas_call x1, Pallas kernels, exchange(): pl.pallas_call(functools.partial(exchange_kernel, pairs, width, hours), o...  41.1 us
    pallas_call x1, Pallas kernels, stack(): pl.pallas_call(functools.partial(stack_kernel, hours), grid_spec=pltpu.Pr...  7.21 us
    pallas_call x1, Pallas kernels, whiten(): pl.pallas_call(whiten_kernel, out_shape=jax.ShapeDtypeStruct((CHUNKS, row...  6.95 us

profile of v2, /device:TPU:1, one launch (start us, length us, event | category | flops | bytes accessed | tf_op | source)
XLA Modules:
  0.0 56.3 jit_solution(3502869818331564237)
XLA Ops:
  0.0 0.0 copy-start.2
  0.0 0.0 copy-start.3
  0.0 0.0 copy-start.1
  0.0 7.0 %whiten.1.w_ref = bf16[2,128,512]{2,1,0:T(8,128)(2,1)} custom-call(bf16[3600,128]{1,0:T(8,128)(2,1)} %bitcast.7, s32[1,128]{1,0:T(1,128)} %bitcast.5, bf16[576,1800]{1,0:T(8,128)(2,1)} %constant.12.clone.even_hbm, bf16[576,1800]{1,0:T(8,128)(2,1)} %constant.13.clone.odd_hbm, bf16[512,576]{1,0:T(8,128)(2,1)} %constant.14.clone.ones_hbm), custom_call_target="tpu_custom_call" | custom-call | tf_op jit(solution)/shard_map/whiten/pallas_call | solution.py:546
  7.0 0.0 copy-done.2
  7.0 0.0 copy-done.3
  7.0 0.0 copy-start
  7.0 0.9 %copy-done = bf16[2,128,512]{2,1,0:T(8,128)(2,1)S(1)} copy-done((bf16[2,128,512]{2,1,0:T(8,128)(2,1)S(1)}, bf16[2,128,512]{2,1,0:T(8,128)(2,1)}, u32[]{:S(2)}) %copy-start) | copy-done | bytes 262168
  7.9 41.1 %exchange.1 = (bf16[4,2,128,512]{3,2,1,0:T(8,128)(2,1)S(1)}, bf16[4,2,32,512]{3,2,1,0:T(8,128)(2,1)S(1)}, s32[8,4,1,128]{3,2,1,0:T(1,128)S(1)}) custom-call(s32[1,2]{1,0:T(1,128)S(1)} %copy-done.3, s32[1,128]{1,0:T(1,128)S(1)} %bitcast.6, bf16[2,128,512]{2,1,0:T(8,128)(2,1)S(1)} %copy-done), custom_call_target="tpu_custom_call" | custom-call | tf_op jit(solution)/shard_map/exchange/pallas_call | solution.py:397
  49.1 0.0 copy-done.1
  49.1 7.2 %stack.1 = f32[1,32,128,256]{3,2,1,0:T(8,128)} custom-call(s32[1]{0:T(128)} %bitcast.me_ref, s32[1,2]{1,0:T(1,128)S(1)} %copy-done.3, bf16[4,2,32,512]{3,2,1,0:T(8,128)(2,1)S(1)} %get-tuple-element.8.bi_ref, bf16[4,2,128,512]{3,2,1,0:T(8,128)(2,1)S(1)} %get-tuple-element.9.bj_ref, s32[8,4,1,128]{3,2,1,0:T(1,128)S(1)} %get-tuple-element.10.ff_ref, ...), custom_call_target="tpu_custom_call" | custom-call | tf_op jit(solution)/shard_map/stack/pallas_call | solution.py:519
Async XLA Ops:
  0.0 7.0 %copy-start.2 = (s32[128,1]{0,1:T(1,128)S(1)}, s32[128,1]{0,1:T(1,128)}, u32[]{:S(2)}) copy-start(s32[128,1]{0,1:T(1,128)} %param.8) | copy-start | bytes 1540
  0.0 7.0 %copy-start.3 = (s32[1,2]{1,0:T(1,128)S(1)}, s32[1,2]{1,0:T(1,128)}, u32[]{:S(2)}) copy-start(s32[1,2]{1,0:T(1,128)} %pair_ref.3) | copy-start | bytes 28
  0.0 49.1 %copy-start.1 = (bf16[1024,256]{1,0:T(8,128)(2,1)S(1)}, bf16[1024,256]{1,0:T(8,128)(2,1)}, u32[]{:S(2)}) copy-start(bf16[1024,256]{1,0:T(8,128)(2,1)} %constant.15.clone.g_ref) | copy-start | bytes 1572868
  7.0 1.0 %copy-start = (bf16[2,128,512]{2,1,0:T(8,128)(2,1)S(1)}, bf16[2,128,512]{2,1,0:T(8,128)(2,1)}, u32[]{:S(2)}) copy-start(bf16[2,128,512]{2,1,0:T(8,128)(2,1)} %whiten.1.w_ref) | copy-start | bytes 786436

commit v3 on v2

--- a/solution.py
+++ b/solution.py
@@ -64,17 +64,11 @@
     return jnp.concatenate([high, low], axis=1)
 
 
-def whiten_kernel(
-    x_ref, use_ref, even_hbm, odd_hbm, ones_hbm, out_ref, even, odd, ones, sem
-):
+def whiten(x_ref, use_ref, even, odd, ones, w_ref, loads):
     stations = x_ref.shape[1]
-    loads = [
-        pltpu.make_async_copy(src, dst, sem.at[k])
-        for k, (src, dst) in enumerate(((even_hbm, even), (odd_hbm, odd), (ones_hbm, ones)))
-    ]
-    for load in loads:
-        load.start()
+    loads[4].wait()
     flags = use_ref[...].astype(jnp.float32)
+    loads[0].wait()
     early = x_ref[:HALF].astype(jnp.float32)
     late = x_ref[HALF:].astype(jnp.float32)
 
@@ -85,12 +79,12 @@
         both = both[:, :stations] + both[:, stations:]
         return both[:HE], both[HE:]
 
-    re_even, im_even = transform(loads[0], even, early + late)
-    re_odd, im_odd = transform(loads[1], odd, early - late)
+    re_even, im_even = transform(loads[1], even, early + late)
+    re_odd, im_odd = transform(loads[2], odd, early - late)
     power = jnp.concatenate(
         [re_even * re_even + im_even * im_even, re_odd * re_odd + im_odd * im_odd], axis=0
     )
-    loads[2].wait()
+    loads[3].wait()
     total = jnp.dot(ones[...], split_hi_lo(power), preferred_element_type=jnp.float32)
     smooth = (total[:, :stations] + total[:, stations:]) * jnp.float32(1.0 / (2 * W + 1))
     weight = flags / jnp.sqrt(smooth + 1e-05)
@@ -100,15 +94,29 @@
         real, imag = (re_even, im_even) if at < HF else (re_odd, im_odd)
         inner = w2 + at % HF
         scale = weight[at : at + CHUNK]
-        out_ref[k, :, :CHUNK] = (real[inner : inner + CHUNK] * scale).T.astype(jnp.bfloat16)
-        out_ref[k, :, CHUNK:] = (imag[inner : inner + CHUNK] * scale).T.astype(jnp.bfloat16)
+        w_ref[k, :, :CHUNK] = (real[inner : inner + CHUNK] * scale).T.astype(jnp.bfloat16)
+        w_ref[k, :, CHUNK:] = (imag[inner : inner + CHUNK] * scale).T.astype(jnp.bfloat16)
 
 
 UNIT = 16
-LAG = 1.6
-
-
-def exchange_kernel(pairs, width, hours, pair_ref, use_ref, w_ref, bj, bi, ff, *scratch):
+LAG = 3.2
+
+
+def exchange_kernel(
+    pairs, width, hours, pair_ref, use_hbm, x_hbm, even_hbm, odd_hbm, ones_hbm, bj, bi, ff,
+    use_ref, x_ref, even, odd, ones, load_sem, w_ref, *scratch
+):
+    loads = [
+        pltpu.make_async_copy(src, dst, load_sem.at[k])
+        for k, (src, dst) in enumerate(
+            (
+                (x_hbm, x_ref), (even_hbm, even), (odd_hbm, odd), (ones_hbm, ones),
+                (use_hbm, use_ref),
+            )
+        )
+    ]
+    for load in loads:
+        load.start()
     rows = w_ref.shape[1]
     depth = pairs // width
     groups = hours // CORES
@@ -154,6 +162,7 @@
             barrier, inc=1, device_id={"pairs": ((z + k) % depth) * width + x},
             device_id_type=MESH,
         )
+    whiten(x_ref, use_ref, even, odd, ones, w_ref, loads)
     pl.semaphore_wait(barrier, width * hours - 1 + depth - 1)
 
     pending = []
@@ -336,7 +345,7 @@
                     {"hours": partner},
                 )
 
-    steps = [(0.0, learn, 0), (LAG + 0.1, flags_row, 0), (2 * LAG + 0.1, flags_column, 0)]
+    steps = [(0.0, learn, 0), (4.0 * LAG, flags_row, 0), (units + 3.0 * LAG, flags_column, 0)]
     steps.append((2 * LAG + 0.2, know, 0))
     stages = [own_row]
     stages += [functools.partial(near_row, d) for d in range(1, depth - 1)]
@@ -384,8 +393,12 @@
                 make().wait_send()
 
 
-def exchange(pair_blocks, flags, whitened, pairs, width, hours):
-    rows, cols = whitened.shape[1:]
+def exchange(pair_blocks, usable, records, pairs, width, hours):
+    rows = records.shape[0]
+    samples = records.reshape(rows, L).T
+    flags = usable.reshape(1, rows)
+    tables = tuple(jnp.asarray(t) for t in (*spectrum_tables(), window_ones()))
+    cols = 2 * CHUNK
     part = rows // hours
     units = CHUNKS * (rows // width // UNIT)
     any_space = pl.BlockSpec(memory_space=pl.ANY)
@@ -401,9 +414,11 @@
             jax.ShapeDtypeStruct((hours, CHUNKS, part, cols), bf16),
             jax.ShapeDtypeStruct((pairs, hours) + flags.shape, flags.dtype),
         ),
-        in_specs=[smem, any_space, any_space],
+        in_specs=[smem] + [pl.BlockSpec(memory_space=pltpu.HBM)] * 5,
         out_specs=(any_space, any_space, any_space),
-        scratch_shapes=[pltpu.VMEM((depth * width + 2 * width, UNIT, cols), bf16)] * units
+        scratch_shapes=[pltpu.VMEM(t.shape, t.dtype) for t in (flags, samples, *tables)]
+        + [dma((5,)), pltpu.VMEM((CHUNKS, rows, cols), bf16)]
+        + [pltpu.VMEM((depth * width + 2 * width, UNIT, cols), bf16)] * units
         + [pltpu.VMEM((2, 2 * width, UNIT, cols), bf16)] * units
         + [pltpu.VMEM((width, 2, UNIT, cols), bf16)] * units
         + [
@@ -438,10 +453,13 @@
             dma((groups, width, units)),
         ],
         compiler_params=pltpu.CompilerParams(
-            collective_id=0, has_side_effects=True, vmem_limit_bytes=32 << 20
+            collective_id=0, has_side_effects=True, vmem_limit_bytes=48 << 20
         ),
         name="exchange",
-    )(pair_blocks, flags, whitened)
+    )(
+        pair_blocks,
+        *(pltpu.with_memory_space_constraint(t, pltpu.HBM) for t in (flags, samples, *tables)),
+    )
 
 
 GROUP = 8
@@ -536,33 +554,12 @@
     )(me, pair_blocks, bi, bj, ff, weights)
 
 
-def whiten(records, usable):
-    rows = records.shape[0]
-    samples = records.reshape(rows, L).T
-    even, odd = spectrum_tables()
-    tables = (jnp.asarray(even), jnp.asarray(odd), jnp.asarray(window_ones()))
-    vmem = pl.BlockSpec(memory_space=pltpu.VMEM)
-    hbm = pl.BlockSpec(memory_space=pltpu.HBM)
-    return pl.pallas_call(
-        whiten_kernel,
-        out_shape=jax.ShapeDtypeStruct((CHUNKS, rows, 2 * CHUNK), jnp.bfloat16),
-        in_specs=[vmem, vmem, hbm, hbm, hbm],
-        out_specs=vmem,
-        scratch_shapes=[pltpu.VMEM(t.shape, t.dtype) for t in tables]
-        + [pltpu.SemaphoreType.DMA((3,))],
-        compiler_params=pltpu.CompilerParams(vmem_limit_bytes=63 << 20),
-        name="whiten",
-    )(samples, usable.reshape(1, rows), *tables)
-
-
 def solution(mesh):
     pairs, hours = mesh.shape["pairs"], mesh.shape["hours"]
     width = 1 << ((pairs.bit_length() - 1) // 2)
 
     def body(records, usable, pair_blocks):
-        whitened = whiten(records, usable)
-        flags = usable.reshape(1, usable.shape[0])
-        bj, bi, ff = exchange(pair_blocks, flags, whitened, pairs, width, hours)
+        bj, bi, ff = exchange(pair_blocks, usable, records, pairs, width, hours)
         me = lax.axis_index("hours").astype(jnp.int32).reshape(1)
         return stack(me, pair_blocks, bi, bj, ff, jnp.asarray(lag_weights()))
 

time: 56.5 us -> 49.3 us (0.87)
  Pallas kernels: 55.3 us -> 48.4 us
    pallas_call x1 -> x0, Pallas kernels: 6.95 us -> none  [whiten(): pl.pallas_call(whiten_kernel, out_shape=jax.ShapeDtypeStruct((CHUNKS, row...]
where the time goes in v3:
time: 49.3 us; the launch traced here: 49.1 us
  Pallas kernels  48.4 us (98%)
  local copies, waits for them, and re-layouts  0.66 us (1%)
    pallas_call x1, Pallas kernels, exchange(): pl.pallas_call(functools.partial(exchange_kernel, pairs, width, hours), o...  41.2 us
    pallas_call x1, Pallas kernels, stack(): pl.pallas_call(functools.partial(stack_kernel, hours), grid_spec=pltpu.Pr...  7.23 us

profile of v3, /device:TPU:1, one launch (start us, length us, event | category | flops | bytes accessed | tf_op | source)
XLA Modules:
  0.0 49.1 jit_solution(1926049178595794404)
XLA Ops:
  0.0 0.0 copy-start.1
  0.0 0.7 %copy-done.1 = s32[1,2]{1,0:T(1,128)S(1)} copy-done((s32[1,2]{1,0:T(1,128)S(1)}, s32[1,2]{1,0:T(1,128)}, u32[]{:S(2)}) %copy-start.1) | copy-done | bytes 32
  0.7 0.0 copy-start
  0.7 41.2 %exchange.1 = (bf16[4,2,128,512]{3,2,1,0:T(8,128)(2,1)S(1)}, bf16[4,2,32,512]{3,2,1,0:T(8,128)(2,1)S(1)}, s32[8,4,1,128]{3,2,1,0:T(1,128)S(1)}) custom-call(s32[1,2]{1,0:T(1,128)S(1)} %copy-done.1, s32[1,128]{1,0:T(1,128)} %bitcast.6, bf16[3600,128]{1,0:T(8,128)(2,1)} %bitcast.5, bf16[576,1800]{1,0:T(8,128)(2,1)} %constant.12.clone.even_hbm, ...), custom_call_target="tpu_custom_call" | custom-call | tf_op jit(solution)/shard_map/exchange/pallas_call | solution.py:410
  41.9 0.0 copy-done
  41.9 7.2 %stack.1 = f32[1,32,128,256]{3,2,1,0:T(8,128)} custom-call(s32[1]{0:T(128)} %bitcast.me_ref, s32[1,2]{1,0:T(1,128)S(1)} %copy-done.1, bf16[4,2,32,512]{3,2,1,0:T(8,128)(2,1)S(1)} %get-tuple-element.8.bi_ref, bf16[4,2,128,512]{3,2,1,0:T(8,128)(2,1)S(1)} %get-tuple-element.9.bj_ref, s32[8,4,1,128]{3,2,1,0:T(1,128)S(1)} %get-tuple-element.10.ff_ref, ...), custom_call_target="tpu_custom_call" | custom-call | tf_op jit(solution)/shard_map/stack/pallas_call | solution.py:537
Async XLA Ops:
  0.0 0.7 %copy-start.1 = (s32[1,2]{1,0:T(1,128)S(1)}, s32[1,2]{1,0:T(1,128)}, u32[]{:S(2)}) copy-start(s32[1,2]{1,0:T(1,128)} %pair_ref.3) | copy-start | bytes 28
  0.7 41.2 %copy-start = (bf16[1024,256]{1,0:T(8,128)(2,1)S(1)}, bf16[1024,256]{1,0:T(8,128)(2,1)}, u32[]{:S(2)}) copy-start(bf16[1024,256]{1,0:T(8,128)(2,1)} %constant.15.clone.g_ref) | copy-start | bytes 1572868
